TPU v7x, 32 devices: a whole 2x2x4 slice. The times are simulated.
32 devices in a mesh: seq: 8 (over z, x), hid: 4 (over y, core).
Axes of the slice: x: 2, y: 2, z: 4, core: 2. Of those that a mesh axis runs over, the one named last changes fastest.
Arguments:
- tokens: bfloat16 [1024, 4096], P('seq', 'hid'), may hold values from -6 to 6
- hidden_grad: bfloat16 [1024, 14336], P('seq', 'hid'), may hold values from -6 to 6
- gate_blocks: bfloat16 [4, 448, 128, 128], P('hid', 'seq'), may hold values from -0.125 to 0.125
- up_blocks: bfloat16 [4, 448, 128, 128], P('hid', 'seq'), may hold values from -0.125 to 0.125
- gate_rows: int32 [4, 448], P('hid'), may hold values from 0 to 31, as said below
- gate_cols: int32 [4, 448], P('hid'), may hold values from 0 to 27
- gate_count: int32 [4], P('hid'), may hold values from 56 to 448, as said below
- up_rows: int32 [4, 448], P('hid'), may hold values from 0 to 31, as said below
- up_cols: int32 [4, 448], P('hid'), may hold values from 0 to 27
- up_count: int32 [4], P('hid'), may hold values from 56 to 448, as said below
Outputs:
- hidden: bfloat16 [1024, 14336], P('seq', 'hid')
- input_grad: bfloat16 [1024, 4096], P('seq', 'hid')
- gate_block_grads: bfloat16 [4, 448, 128, 128], P('hid', 'seq')
- up_block_grads: bfloat16 [4, 448, 128, 128], P('hid', 'seq')
Inputs may be any that keep to these rules, and one draw needn't show every extreme that they name: For each panel, the pairs (gate_rows, gate_cols) over all 448 slots are distinct. `gate_count`: slots at or after a panel's count hold no block of the matrix. For each panel, the pairs (up_rows, up_cols) over all 448 slots are distinct. `up_count`: slots at or after a panel's count hold no block of the matrix.
All inputs are finite; a program needn't handle non-finite values.
Results may differ from a plain program's by a relative error of at most 0.018.
Values may be sent and summed in bfloat16 or wider, within the bound.
A program may use at most 192 MiB of HBM per device.

v0:
```python
import math
import jax
import jax.numpy as jnp
from jax import lax
from jax.sharding import PartitionSpec as P


def swapped(value, axis, stride):
    mask = 2**stride
    pairs = [(source, source ^ mask) for source in range(lax.axis_size(axis))]
    return lax.ppermute(value, axis, pairs)


def silu_parts(preact):
    sigma = jax.nn.sigmoid(preact)
    return (preact * sigma, sigma * (1.0 + preact * (1.0 - sigma)))


def place_split(products, placing, form):
    high_part = products.astype(jnp.bfloat16)
    rest_part = (products - high_part.astype(jnp.float32)).astype(jnp.bfloat16)
    table = placing.astype(jnp.bfloat16)
    placed = jnp.einsum(form, high_part, table, preferred_element_type=jnp.float32)
    return placed + jnp.einsum(form, rest_part, table, preferred_element_type=jnp.float32)


def project_slots(tiles, weights, rows, columns, live_count, group_size, trips, col_blocks):
    tok_rows = tiles.shape[0]
    block_size = tiles.shape[2]
    targets = jnp.arange(col_blocks)
    offsets = jnp.arange(group_size)

    def project_one_group(group_index, running):
        start = group_index * group_size
        chosen = lax.dynamic_slice_in_dim(weights, start, group_size, 0)
        row_ids = lax.dynamic_slice_in_dim(rows, start, group_size, 0)
        col_ids = lax.dynamic_slice_in_dim(columns, start, group_size, 0)
        active = start + offsets < live_count
        picked = jnp.take(tiles, row_ids, axis=1)
        products = jnp.einsum("tsk,skn->tsn", picked, chosen, preferred_element_type=jnp.float32)
        placing = (col_ids[:, None] == targets[None, :]) & active[:, None]
        return running + place_split(products, placing, "tsn,sc->tcn")

    initial = jnp.zeros((tok_rows, col_blocks, block_size), jnp.float32)
    return lax.fori_loop(0, trips, project_one_group, initial)


def return_slots(grad_tiles, weights, rows, columns, live_count, group_size, trips, row_blocks):
    tok_rows = grad_tiles.shape[0]
    block_size = grad_tiles.shape[2]
    targets = jnp.arange(row_blocks)
    offsets = jnp.arange(group_size)

    def return_one_group(group_index, running):
        start = group_index * group_size
        chosen = lax.dynamic_slice_in_dim(weights, start, group_size, 0)
        row_ids = lax.dynamic_slice_in_dim(rows, start, group_size, 0)
        col_ids = lax.dynamic_slice_in_dim(columns, start, group_size, 0)
        active = start + offsets < live_count
        picked = jnp.take(grad_tiles, col_ids, axis=1)
        products = jnp.einsum("tsn,skn->tsk", picked, chosen, preferred_element_type=jnp.float32)
        placing = (row_ids[:, None] == targets[None, :]) & active[:, None]
        return running + place_split(products, placing, "tsk,sr->trk")

    initial = jnp.zeros((tok_rows, row_blocks, block_size), jnp.float32)
    return lax.fori_loop(0, trips, return_one_group, initial)


def on_device(
    tokens,
    hidden_grad,
    gate_blocks,
    up_blocks,
    gate_rows,
    gate_cols,
    gate_count,
    up_rows,
    up_cols,
    up_count,
):
    gathered = lax.all_gather(tokens, "hid", axis=1, tiled=True)
    tok_rows = gathered.shape[0]
    block_size = gate_blocks.shape[2]
    row_blocks = gathered.shape[1] // block_size
    col_blocks = hidden_grad.shape[1] // block_size
    gate_all = lax.all_gather(gate_blocks, "seq", axis=1, tiled=True)
    up_all = lax.all_gather(up_blocks, "seq", axis=1, tiled=True)
    capacity = gate_all.shape[1]
    group_size = 32
    groups = capacity // group_size
    gate_live = gate_count[0]
    up_live = up_count[0]
    tiles = gathered.reshape(tok_rows, row_blocks, block_size)
    gate_pre = project_slots(
        tiles, gate_all[0], gate_rows[0], gate_cols[0], gate_live, group_size, groups, col_blocks
    )
    up_pre = project_slots(
        tiles, up_all[0], up_rows[0], up_cols[0], up_live, group_size, groups, col_blocks
    )
    activated, slope = silu_parts(gate_pre)
    hidden = (activated * up_pre).astype(jnp.bfloat16)
    upstream = hidden_grad.reshape(tok_rows, col_blocks, block_size).astype(jnp.float32)
    gate_grad = (upstream * up_pre * slope).astype(jnp.bfloat16)
    up_grad = (upstream * activated).astype(jnp.bfloat16)
    input_sum = return_slots(
        gate_grad,
        gate_all[0],
        gate_rows[0],
        gate_cols[0],
        gate_live,
        group_size,
        groups,
        row_blocks,
    )
    input_sum = input_sum + return_slots(
        up_grad, up_all[0], up_rows[0], up_cols[0], up_live, group_size, groups, row_blocks
    )
    input_grad = lax.psum_scatter(
        input_sum.reshape(tok_rows, row_blocks * block_size).astype(jnp.bfloat16),
        "hid",
        scatter_dimension=1,
        tiled=True,
    )
    seq_count = lax.axis_size("seq")
    position = lax.axis_index("seq")
    levels = seq_count.bit_length() - 1
    blk_dev = capacity // seq_count
    other_tiles, other_gate, other_up = swapped((tiles, gate_grad, up_grad), "seq", 0)
    both_tiles = jnp.concatenate([tiles, other_tiles], axis=0)
    both_gate = jnp.concatenate([gate_grad, other_gate], axis=0)
    both_up = jnp.concatenate([up_grad, other_up], axis=0)
    parity = position % 2
    owners = 2 * jnp.arange(seq_count // 2) + parity
    slot_ids = (owners[:, None] * blk_dev + jnp.arange(blk_dev)[None, :]).reshape(-1)
    stacked = []
    for rows, columns, live_count, grad_tiles in (
        (gate_rows[0], gate_cols[0], gate_live, both_gate),
        (up_rows[0], up_cols[0], up_live, both_up),
    ):
        row_ids = jnp.take(rows, slot_ids)
        col_ids = jnp.take(columns, slot_ids)
        picked_input = jnp.take(both_tiles, row_ids, axis=1)
        picked_grad = jnp.take(grad_tiles, col_ids, axis=1)
        block_term = jnp.einsum(
            "tsk,tsn->skn", picked_input, picked_grad, preferred_element_type=jnp.float32
        )
        stacked.append(block_term * (slot_ids < live_count).astype(jnp.float32)[:, None, None])
    current = jnp.stack(stacked, axis=1)
    current = current.reshape((seq_count // 2, blk_dev) + current.shape[1:])
    for level in range(1, levels):
        own_bit = position // 2**level % 2
        halves = current.reshape((current.shape[0] // 2, 2) + current.shape[1:])
        kept = lax.dynamic_index_in_dim(halves, own_bit, 1, keepdims=False)
        sent = lax.dynamic_index_in_dim(halves, 1 - own_bit, 1, keepdims=False)
        received = swapped(sent.astype(jnp.bfloat16), "seq", level)
        current = kept + received.astype(jnp.float32)
    summed = current[0]
    scale = 1.0 / math.sqrt(tok_rows * seq_count)
    gate_block_grads = (summed[:, 0] * scale).astype(jnp.bfloat16)[None]
    up_block_grads = (summed[:, 1] * scale).astype(jnp.bfloat16)[None]
    return (
        hidden.reshape(tok_rows, col_blocks * block_size),
        input_grad,
        gate_block_grads,
        up_block_grads,
    )


def solution(mesh):
    placed = (
        P("seq", "hid"),
        P("seq", "hid"),
        P("hid", "seq", None, None),
        P("hid", "seq", None, None),
        P("hid", None),
        P("hid", None),
        P("hid"),
        P("hid", None),
        P("hid", None),
        P("hid"),
    )
    return jax.shard_map(
        on_device,
        mesh=mesh,
        in_specs=placed,
        out_specs=(
            P("seq", "hid"),
            P("seq", "hid"),
            P("hid", "seq", None, None),
            P("hid", "seq", None, None),
        ),
        check_vma=False,
    )
```

profile of v0, /device:TPU:0, one launch (start us, length us, event | category | flops | bytes accessed | tf_op | source)
XLA Modules:
  0.0 1165.3 jit_solution(1844786483724718215)
XLA Ops:
  16.3 13.3 %all-gather.6.cloned.1.call-done = bf16[128,4096]{0,1:T(8,128)(2,1)} async-done(((bf16[128,1024]{0,1:T(8,128)(2,1)}), bf16[128,4096]{0,1:T(8,128)(2,1)}) %all-gather.6.cloned.1.call-update) | async-done | bytes 1048592 | tf_op jit(solution)/shard_map/all_gather | solution.py:81
  33.3 200.2 %all-gather.8.cloned.1.call-done = bf16[1,448,128,128]{3,2,0,1:T(8,128)(2,1)} async-done(((bf16[1,56,128,128]{3,2,0,1:T(8,128)(2,1)}), bf16[1,448,128,128]{3,2,0,1:T(8,128)(2,1)}) %all-gather.8.cloned.1.call-update) | async-done | bytes 14680080 | tf_op jit(solution)/shard_map/all_gather | solution.py:87
  233.5 192.3 %while.61 = (s32[]{:T(128)}, f32[128,28,128]{2,1,0:T(8,128)}, s32[448]{0:T(512)S(1)}, s32[]{:T(128)}, bf16[448,128,128]{2,1,0:T(8,128)(2,1)}, /*index=5*/s32[448...) while((s32[]{:T(128)}, f32[128,28,128]{2,1,0:T(8,128)}, ...), condition=%wide.region_3.5_spmd.clone, body=%wide.region_2.4_spmd.clone.sunk | while | flops 196940544 | bytes 19928416 | solution.py:45
  311.5 4.6 bitcast_add_fusion.9
  394.6 3.9 bitcast_add_fusion.9
  425.8 9.8 all-gather.4.cloned.1.call-done
  435.6 193.2 %while.60 = (s32[]{:T(128)}, f32[128,28,128]{2,1,0:T(8,128)}, s32[448]{0:T(512)S(1)}, s32[]{:T(128)}, bf16[448,128,128]{2,1,0:T(8,128)(2,1)}, /*index=5*/s32[448...) while((s32[]{:T(128)}, f32[128,28,128]{2,1,0:T(8,128)}, ...), condition=%wide.region_1.3_spmd.clone, body=%wide.region_0.2_spmd.clone.sunk | while | flops 196940544 | bytes 19928416 | solution.py:45
  569.6 3.8 bitcast_add_fusion.8
  628.8 6.5 multiply_convert_fusion.1
  645.1 9.4 gather_fusion.5
  654.5 9.2 gather_fusion.9
  665.3 9.2 gather_fusion.7
  678.0 9.1 gather_fusion.11
  687.2 18.4 %fusion.105 = f32[224,128,128]{2,1,0:T(8,128)} fusion(bf16[224,256,128]{2,1,0:T(8,128)(2,1)} %gather_fusion.7, pred[224]{0:T(512)(128)(4,1)S(1)} %get-tuple-element.961, bf16[224,256,128]{2,1,0:T(8,128)(2,1)} %gather_fusion.5, pred[224]{0:T(512)(128)(4,1)S(1)} %get-tuple-element.963, f32[224]{0:T(256)S(1)} %get-tuple-element.960), kind=kOutput, calls=%fused_computation.141 | convolution fusion | flops 1897398272 | bytes 44041536 | tf_op jit(solution)/shard_map/tsk,tsn->skn/dot_general | solution.py:144
  705.6 18.5 %fusion.110 = f32[224,128,128]{2,1,0:T(8,128)} fusion(bf16[224,256,128]{2,1,0:T(8,128)(2,1)} %gather_fusion.11, pred[224]{0:T(512)(128)(4,1)S(1)} %get-tuple-element.944, bf16[224,256,128]{2,1,0:T(8,128)(2,1)} %gather_fusion.9, pred[224]{0:T(512)(128)(4,1)S(1)} %get-tuple-element.941, f32[224]{0:T(256)S(1)} %get-tuple-element.959), kind=kOutput, calls=%fused_computation.142 | convolution fusion | flops 1897398272 | bytes 44041536 | tf_op jit(solution)/shard_map/tsk,tsn->skn/dot_general | solution.py:144
  724.1 10.1 fusion.115
  734.2 192.1 %while.62 = (s32[]{:T(128)}, f32[128,32,128]{2,1,0:T(8,128)}, s32[448]{0:T(512)S(1)}, s32[]{:T(128)}, bf16[448,128,128]{2,1,0:T(8,128)(2,1)}, /*index=5*/s32[448...) while((s32[]{:T(128)}, f32[128,32,128]{2,1,0:T(8,128)}, ...), condition=%wide.region_5.8_spmd.clone.clone, body=%wide.region_4.0_spmd.clone.clone.sunk | while | flops 205526272 | bytes 20976992 | solution.py:66
  757.1 3.9 bitcast_add_fusion.10
  770.9 3.9 bitcast_add_fusion.10
  784.7 3.9 bitcast_add_fusion.10
  798.5 3.9 bitcast_add_fusion.10
  812.2 3.9 bitcast_add_fusion.10
  826.0 3.9 bitcast_add_fusion.10
  839.8 3.9 bitcast_add_fusion.10
  853.5 3.9 bitcast_add_fusion.10
  867.3 3.9 bitcast_add_fusion.10
  881.1 3.9 bitcast_add_fusion.10
  894.8 3.9 bitcast_add_fusion.10
  908.6 3.9 bitcast_add_fusion.10
  922.4 3.9 bitcast_add_fusion.10
  926.2 8.6 fusion.90
  934.9 5.1 copy-done.7
  945.5 186.0 %while.63 = (s32[]{:T(128)}, f32[128,32,128]{2,1,0:T(8,128)}, s32[448]{0:T(512)}, s32[]{:T(128)}, bf16[448,128,128]{2,1,0:T(8,128)(2,1)}, /*index=5*/s32[448]{0:...) while((s32[]{:T(128)}, f32[128,32,128]{2,1,0:T(8,128)}, ...), condition=%wide.region_7.10_spmd.clone.clone, body=%wide.region_6.9_spmd.clone.clone.sunk | while | flops 205526272 | bytes 24647044 | solution.py:66
  967.5 3.9 bitcast_add_fusion.11
  980.9 3.9 bitcast_add_fusion.11
  994.2 3.9 bitcast_add_fusion.11
  1007.5 3.9 bitcast_add_fusion.11
  1020.9 3.9 bitcast_add_fusion.11
  1034.2 3.9 bitcast_add_fusion.11
  1047.5 3.9 bitcast_add_fusion.11
  1060.8 3.9 bitcast_add_fusion.11
  1074.2 3.9 bitcast_add_fusion.11
  1087.5 3.9 bitcast_add_fusion.11
  1100.8 3.9 bitcast_add_fusion.11
  1114.2 3.9 bitcast_add_fusion.11
  1127.5 3.9 bitcast_add_fusion.11
  1137.6 5.8 add_bitcast_fusion
  1146.2 12.6 %reduce-scatter.2.cloned.1.call-done = bf16[128,1024]{1,0:T(8,128)(2,1)} async-done(((bf16[128,4096]{1,0:T(8,128)(2,1)}), bf16[128,1024]{1,0:T(8,128)(2,1)}) %reduce-scatter.2.cloned.1.call-update) | async-done | bytes 262160 | tf_op jit(solution)/shard_map/reduce_scatter | solution.py:118
  (569 shorter events, 689.1 us)
Async XLA Ops:
  7.2 22.4 %all-gather.6.cloned.1.call-start = ((), (), s32[]{:S(2)}) async-start(), calls=%async_computation.2 | async-start | bytes 1310720 | tf_op jit(solution)/shard_map/all_gather | solution.py:81
  9.0 1.6 copy-start.9
  9.0 224.4 %all-gather.8.cloned.1.call-start = ((), (), s32[]{:S(2)}) async-start(), calls=%async_computation.3 | async-start | bytes 16515072 | tf_op jit(solution)/shard_map/all_gather | solution.py:87
  9.8 425.8 %all-gather.4.cloned.1.call-start = ((), (), s32[]{:S(2)}) async-start(), calls=%async_computation.1 | async-start | bytes 16515072 | tf_op jit(solution)/shard_map/all_gather | solution.py:86
  10.5 1148.3 %reduce-scatter.2.cloned.1.call-start = ((), (), s32[]{:S(2)}) async-start(), calls=%async_computation.4 | async-start | bytes 1310720 | tf_op jit(solution)/shard_map/reduce_scatter | solution.py:118
  10.6 3.7 copy-start.3
  12.8 220.6 %copy-start.2 = (s32[1,448]{1,0:T(1,128)S(1)}, s32[1,448]{1,0:T(1,128)}, u32[]{:S(2)}) copy-start(s32[1,448]{1,0:T(1,128)} %param.36) | copy-start | bytes 5380
  31.8 611.6 %collective-permute-start = (bf16[128,32,128]{2,0,1:T(8,128)(2,1)}, bf16[128,32,128]{2,0,1:T(8,128)(2,1)}, u32[]{:S(2)}, u32[]{:S(2)}) collective-permute-start(bf16[128,32,128]{2,0,1:T(8,128)(2,1)} %copy.98), channel_id=1, source_target_pairs={{0,4},{4,0},{8,12},{12,8},{16,20},{20,16},{24,28},{28,24},{1,5},{5... | collective-permute-start | bytes 3145736 | tf_op jit(solution)/shard_map/ppermute | solution.py:11
  233.5 202.1 %copy-start = (s32[1,448]{1,0:T(1,128)S(1)}, s32[1,448]{1,0:T(1,128)}, u32[]{:S(2)}) copy-start(s32[1,448]{1,0:T(1,128)} %param.33) | copy-start | bytes 5380
  233.5 202.1 %copy-start.1 = (s32[1,448]{1,0:T(1,128)S(1)}, s32[1,448]{1,0:T(1,128)}, u32[]{:S(2)}) copy-start(s32[1,448]{1,0:T(1,128)} %param.32) | copy-start | bytes 5380
  635.3 41.4 %copy-start.4 = (bf16[128,28,128]{2,0,1:T(8,128)(2,1)}, bf16[128,28,128]{2,0,1:T(8,128)(2,1)S(1)}, u32[]{:S(2)}) copy-start(bf16[128,28,128]{2,0,1:T(8,128)(2,1)S(1)} %get-tuple-element.1284) | copy-start | bytes 2752516
  635.3 28.4 %collective-permute-start.1 = (bf16[128,28,128]{2,0,1:T(8,128)(2,1)}, bf16[128,28,128]{2,0,1:T(8,128)(2,1)}, u32[]{:S(2)}, u32[]{:S(2)}) collective-permute-start(bf16[128,28,128]{2,0,1:T(8,128)(2,1)} %get-tuple-element.1251), channel_id=1, source_target_pairs={{0,4},{4,0},{8,12},{12,8},{16,20},{20,16},{24,28},{28,24},{1,5},{5... | collective-permute-start | bytes 2752520 | tf_op jit(solution)/shard_map/ppermute | solution.py:11
  635.9 40.8 %collective-permute-start.2 = (bf16[128,28,128]{2,0,1:T(8,128)(2,1)S(1)}, bf16[128,28,128]{2,0,1:T(8,128)(2,1)}, u32[]{:S(2)}, u32[]{:S(2)}) collective-permute-start(bf16[128,28,128]{2,0,1:T(8,128)(2,1)S(1)} %get-tuple-element.1284), channel_id=1, source_target_pairs={{0,4},{4,0},{8,12},{12,8},{16,20},{20,16},{24,28},{28,24},{1,5},{5... | collective-permute-start | bytes 2752520 | tf_op jit(solution)/shard_map/ppermute | solution.py:11
  734.2 192.1 %collective-permute-start.3 = (bf16[2,56,2,128,128]{4,3,1,2,0:T(8,128)(2,1)}, bf16[2,56,2,128,128]{4,3,1,2,0:T(8,128)(2,1)}, u32[]{:S(2)}, u32[]{:S(2)}) collective-permute-start(bf16[2,56,2,128,128]{4,3,1,2,0:T(8,128)(2,1)} %fusion.115), channel_id=1, source_target_pairs={{0,8},{4,12},{8,0},{12,4},{16,24},{20,28},{24,16},{28,20},{1,9},{5... | collective-permute-start | bytes 22020104 | tf_op jit(solution)/shard_map/ppermute | solution.py:11
  934.9 5.1 copy-start.7
  940.0 5.5 copy-start.5
  942.7 194.9 %collective-permute-start.4 = (bf16[1,56,2,128,128]{4,3,1,2,0:T(8,128)(2,1)}, bf16[1,56,2,128,128]{4,3,1,2,0:T(8,128)(2,1)}, u32[]{:S(2)}, u32[]{:S(2)}) collective-permute-start(bf16[1,56,2,128,128]{4,3,1,2,0:T(8,128)(2,1)} %dynamic-slice_convert_fusion), channel_id=1, source_target_pairs={{0,16},{4,20},{8,24},{12,28},{16,0},{20,4},{24,8},{28,12},{1,17},{... | collective-permute-start | bytes 11010056 | tf_op jit(solution)/shard_map/ppermute | solution.py:11
  954.9 3.3 copy-start.6
  967.5 3.9 copy-start.6
  980.9 3.9 copy-start.6
  994.2 3.9 copy-start.6
  1007.5 3.9 copy-start.6
  1020.9 3.9 copy-start.6
  1034.2 3.9 copy-start.6
  1047.5 3.9 copy-start.6
  1060.8 3.9 copy-start.6
  1074.2 3.9 copy-start.6
  1087.5 3.9 copy-start.6
  1100.8 3.9 copy-start.6
  1114.2 3.9 copy-start.6
  1127.5 3.9 copy-start.6
  1134.1 1.5 copy-start.8
Sparse Core Ops, SparseCore 0:
  10.1 19.4 all-gather.5
  31.8 201.6 all-gather.7
  235.7 199.8 all-gather.3
  1135.7 23.0 reduce-scatter.1
where the time goes:
time: 1170 us
  matrix products  462 us (39%)
  local copies, waits for them, and re-layouts  359 us (31%)
  waiting for transfers between devices  239 us (20%)
  other arithmetic  82.2 us (7%)
  between operations  15.4 us (1%)
    dot_general x56, matrix products, place_split(): jnp.einsum(form, rest_part, table, preferred_element_type=jnp.float32)  213 us
    all_gather x1, waiting for transfers between devices, on_device(): up_all = lax.all_gather(up_blocks, 'seq', axis=1, tiled=True)  200 us
    convert_element_type x56, local copies, waits for them, and re-layouts, place_split(): rest_part = (products - high_part.astype(jnp.float32)).astype(jnp.bfloat16)  95.1 us
    convert_element_type x56, local copies, waits for them, and re-layouts, place_split(): high_part = products.astype(jnp.bfloat16)  95 us
    dot_general x56, matrix products, place_split(): jnp.einsum(form, high_part, table, preferred_element_type=jnp.float32)  91.5 us
    dot_general x28, matrix products, return_one_group(): jnp.einsum('tsn,skn->tsk', picked, chosen, preferred_element_type=jnp.flo...  60.6 us
    dot_general x28, matrix products, project_one_group(): jnp.einsum('tsk,skn->tsn', picked, chosen, preferred_element_type=jnp.flo...  59.6 us
    gather x28, local copies, waits for them, and re-layouts, project_one_group(): picked = jnp.take(tiles, row_ids, axis=1)  55.3 us
  transfers between devices with their start and end apart: 9, of which 5 were waited for; matrix products, arithmetic and copies ran while one was open for 71% of the time, Pallas kernels for 0%

commit v1 on v0

--- a/solution.py
+++ b/solution.py
@@ -3,6 +3,28 @@
 import jax.numpy as jnp
 from jax import lax
 from jax.sharding import PartitionSpec as P
+
+
+def in_order(blocks, dim):
+    lengths = list(blocks.shape[1:])
+    lengths[dim] *= blocks.shape[0]
+    return jnp.moveaxis(blocks, 0, dim).reshape(lengths)
+
+
+def ring_gather(x, axis, dim):
+    length = lax.axis_size(axis)
+    pairs = [(i, (i + 1) % length) for i in range(length)]
+    back = [(b, a) for a, b in pairs]
+    lower, upper = ([], [])
+    for step in range(length - 1):
+        if step % 2 == 0:
+            lower.append(lax.ppermute(lower[-1] if lower else x, axis, pairs))
+        else:
+            upper.append(lax.ppermute(upper[-1] if upper else x, axis, back))
+    pieces = jnp.stack([*lower[::-1], x, *upper])
+    shift = lax.axis_index(axis) - len(lower)
+    pieces = pieces[(jnp.arange(length) - shift) % length]
+    return in_order(pieces, dim)
 
 
 def swapped(value, axis, stride):
@@ -84,7 +106,7 @@
     row_blocks = gathered.shape[1] // block_size
     col_blocks = hidden_grad.shape[1] // block_size
     gate_all = lax.all_gather(gate_blocks, "seq", axis=1, tiled=True)
-    up_all = lax.all_gather(up_blocks, "seq", axis=1, tiled=True)
+    up_all = ring_gather(up_blocks, "seq", 1)
     capacity = gate_all.shape[1]
     group_size = 32
     groups = capacity // group_size

time: 1170 us -> 1340 us (1.15)
  waiting for transfers between devices: 239 us -> 375 us
  starting transfers between devices: 6.42 us -> 29 us
  local copies, waits for them, and re-layouts: 359 us -> 376 us
    ppermute x0 -> x7, waiting for transfers between devices: none -> 362 us  [the longest x4 347 us: ring_gather(): lower.append(lax.ppermute(lower[-1] if lower else x, axis, pairs))]
    all_gather x1 -> x0, waiting for transfers between devices: 200 us -> none  [on_device(): up_all = lax.all_gather(up_blocks, 'seq', axis=1, tiled=True)]
    ppermute x0 -> x7, starting transfers between devices: none -> 22.5 us  [the longest x3 13.8 us: ring_gather(): upper.append(lax.ppermute(upper[-1] if upper else x, axis, back))]
    unnamed x23 -> x36, local copies, waits for them, and re-layouts: 12.6 us -> 29.1 us
  transfers between devices with their start and end apart: 9 -> 15, of which waited for: 5 -> 9; matrix products, arithmetic and copies ran while one was open for 71% -> 62% of each run, Pallas kernels for 0% -> 0%
where the time goes in v1:
time: 1340 us; the launch traced here: 1330 us
  matrix products  453 us (34%)
  local copies, waits for them, and re-layouts  376 us (28%)
  waiting for transfers between devices  375 us (28%)
  other arithmetic  82.4 us (6%)
  starting transfers between devices  29 us (2%)
  between operations  15.6 us (1%)
    ppermute x4, waiting for transfers between devices, ring_gather(): lower.append(lax.ppermute(lower[-1] if lower else x, axis, pairs))  347 us
    dot_general x56, matrix products, place_split(): jnp.einsum(form, rest_part, table, preferred_element_type=jnp.float32)  205 us
    convert_element_type x56, local copies, waits for them, and re-layouts, place_split(): rest_part = (products - high_part.astype(jnp.float32)).astype(jnp.bfloat16)  93.8 us
    convert_element_type x56, local copies, waits for them, and re-layouts, place_split(): high_part = products.astype(jnp.bfloat16)  93.8 us
    dot_general x56, matrix products, place_split(): jnp.einsum(form, high_part, table, preferred_element_type=jnp.float32)  91.5 us
    dot_general x28, matrix products, return_one_group(): jnp.einsum('tsn,skn->tsk', picked, chosen, preferred_element_type=jnp.flo...  60.3 us
    dot_general x28, matrix products, project_one_group(): jnp.einsum('tsk,skn->tsn', picked, chosen, preferred_element_type=jnp.flo...  59.5 us
    gather x28, local copies, waits for them, and re-layouts, project_one_group(): picked = jnp.take(tiles, row_ids, axis=1)  55.2 us
  transfers between devices with their start and end apart: 15, of which 9 were waited for; matrix products, arithmetic and copies ran while one was open for 62% of the time, Pallas kernels for 0%

profile of v1, /device:TPU:0, one launch (start us, length us, event | category | flops | bytes accessed | tf_op | source)
XLA Modules:
  0.0 1332.6 jit_solution(17125275692493648881)
XLA Ops:
  12.8 48.0 %collective-permute-done = bf16[1,56,128,128]{3,2,1,0:T(8,128)(2,1)S(1)} collective-permute-done((bf16[1,56,128,128]{3,2,1,0:T(8,128)(2,1)}, bf16[1,56,128,128]{3,2,1,0:T(8,128)(2,1)S(1)}, u32[]{:S(2)}, u32[]{:S(2)}) %collective-permute-start) | collective-permute-done | bytes 1835040 | tf_op jit(solution)/shard_map/ppermute | solution.py:21
  61.5 4.1 collective-permute-start.4
  65.6 82.4 %collective-permute-done.1 = bf16[1,56,128,128]{3,2,1,0:T(8,128)(2,1)S(1)} collective-permute-done((bf16[1,56,128,128]{3,2,1,0:T(8,128)(2,1)S(1)}, bf16[1,56,128,128]{3,2,1,0:T(8,128)(2,1)S(1)}, u32[]{:S(2)}, u32[]{:S(2)}) %collective-permute-start.1) | collective-permute-done | bytes 1835040 | tf_op jit(solution)/shard_map/ppermute | solution.py:21
  154.8 114.2 %collective-permute-done.2 = bf16[1,56,128,128]{3,2,1,0:T(8,128)(2,1)} collective-permute-done((bf16[1,56,128,128]{3,2,1,0:T(8,128)(2,1)S(1)}, bf16[1,56,128,128]{3,2,1,0:T(8,128)(2,1)}, u32[]{:S(2)}, u32[]{:S(2)}) %collective-permute-start.2) | collective-permute-done | bytes 1835040 | tf_op jit(solution)/shard_map/ppermute | solution.py:21
  279.1 6.8 collective-permute-start.6
  286.0 102.4 %collective-permute-done.3 = bf16[1,56,128,128]{3,2,1,0:T(8,128)(2,1)} collective-permute-done((bf16[1,56,128,128]{3,2,1,0:T(8,128)(2,1)}, bf16[1,56,128,128]{3,2,1,0:T(8,128)(2,1)}, u32[]{:S(2)}, u32[]{:S(2)}) %collective-permute-start.3) | collective-permute-done | bytes 1835040 | tf_op jit(solution)/shard_map/ppermute | solution.py:21
  397.5 14.6 %collective-permute-done.6 = bf16[1,56,128,128]{3,2,1,0:T(8,128)(2,1)S(1)} collective-permute-done((bf16[1,56,128,128]{3,2,1,0:T(8,128)(2,1)}, bf16[1,56,128,128]{3,2,1,0:T(8,128)(2,1)S(1)}, u32[]{:S(2)}, u32[]{:S(2)}) %collective-permute-start.6) | collective-permute-done | bytes 1835040 | tf_op jit(solution)/shard_map/ppermute | solution.py:23
  412.3 5.2 copy-done.8
  417.5 12.9 gather_fusion.4
  430.5 190.1 %while.61 = (s32[]{:T(128)}, f32[128,28,128]{2,1,0:T(8,128)}, s32[448]{0:T(512)S(1)}, s32[]{:T(128)}, bf16[448,128,128]{2,1,0:T(8,128)(2,1)}, /*index=5*/s32[448...) while((s32[]{:T(128)}, f32[128,28,128]{2,1,0:T(8,128)}, ...), condition=%wide.region_3.5_spmd.clone, body=%wide.region_2.4_spmd.clone.sunk | while | flops 196940544 | bytes 19928416 | solution.py:67
  453.4 3.7 bitcast_add_fusion.9
  467.0 3.7 bitcast_add_fusion.9
  480.6 3.7 bitcast_add_fusion.9
  494.3 3.7 bitcast_add_fusion.9
  507.9 3.7 bitcast_add_fusion.9
  521.5 3.7 bitcast_add_fusion.9
  535.1 3.7 bitcast_add_fusion.9
  548.8 3.7 bitcast_add_fusion.9
  562.4 3.7 bitcast_add_fusion.9
  620.6 189.9 %while.60 = (s32[]{:T(128)}, f32[128,28,128]{2,1,0:T(8,128)}, s32[448]{0:T(512)S(1)}, s32[]{:T(128)}, bf16[448,128,128]{2,1,0:T(8,128)(2,1)}, /*index=5*/s32[448...) while((s32[]{:T(128)}, f32[128,28,128]{2,1,0:T(8,128)}, ...), condition=%wide.region_1.3_spmd.clone, body=%wide.region_0.2_spmd.clone.sunk | while | flops 196940544 | bytes 19928416 | solution.py:67
  810.5 6.6 multiply_convert_fusion.1
  828.8 9.4 gather_fusion.6
  838.2 9.2 gather_fusion.10
  849.1 9.2 gather_fusion.8
  860.1 9.1 gather_fusion.12
  869.3 18.2 %fusion.105 = f32[224,128,128]{2,1,0:T(8,128)} fusion(bf16[224,256,128]{2,1,0:T(8,128)(2,1)} %gather_fusion.8, pred[224]{0:T(512)(128)(4,1)S(1)} %get-tuple-element.961, bf16[224,256,128]{2,1,0:T(8,128)(2,1)} %gather_fusion.6, pred[224]{0:T(512)(128)(4,1)S(1)} %get-tuple-element.963, f32[224]{0:T(256)S(1)} %get-tuple-element.960), kind=kOutput, calls=%fused_computation.142 | convolution fusion | flops 1897398272 | bytes 44041536 | tf_op jit(solution)/shard_map/tsk,tsn->skn/dot_general | solution.py:166
  887.5 18.4 %fusion.110 = f32[224,128,128]{2,1,0:T(8,128)} fusion(bf16[224,256,128]{2,1,0:T(8,128)(2,1)} %gather_fusion.12, pred[224]{0:T(512)(128)(4,1)S(1)} %get-tuple-element.944, bf16[224,256,128]{2,1,0:T(8,128)(2,1)} %gather_fusion.10, pred[224]{0:T(512)(128)(4,1)S(1)} %get-tuple-element.941, f32[224]{0:T(256)S(1)} %get-tuple-element.959), kind=kOutput, calls=%fused_computation.143 | convolution fusion | flops 1897398272 | bytes 44041536 | tf_op jit(solution)/shard_map/tsk,tsn->skn/dot_general | solution.py:166
  906.0 10.1 fusion.115
  916.1 189.2 %while.62 = (s32[]{:T(128)}, f32[128,32,128]{2,1,0:T(8,128)}, s32[448]{0:T(512)S(1)}, s32[]{:T(128)}, bf16[448,128,128]{2,1,0:T(8,128)(2,1)}, /*index=5*/s32[448...) while((s32[]{:T(128)}, f32[128,32,128]{2,1,0:T(8,128)}, ...), condition=%wide.region_5.8_spmd.clone.clone, body=%wide.region_4.7_spmd.clone.clone.sunk | while | flops 205526272 | bytes 20976992 | solution.py:88
  1105.3 8.6 fusion.90
  1113.9 5.2 copy-done.7
  1121.8 3.8 collective-permute-start.11
  1125.6 173.6 %while.63 = (s32[]{:T(128)}, f32[128,32,128]{2,1,0:T(8,128)}, s32[448]{0:T(512)S(1)}, s32[]{:T(128)}, bf16[448,128,128]{2,1,0:T(8,128)(2,1)}, /*index=5*/s32[448...) while((s32[]{:T(128)}, f32[128,32,128]{2,1,0:T(8,128)}, ...), condition=%wide.region_7.10_spmd.clone.clone, body=%wide.region_6.9_spmd.clone.clone.sunk | while | flops 205526272 | bytes 24647044 | solution.py:88
  1146.1 3.7 bitcast_add_fusion.11
  1158.6 3.7 bitcast_add_fusion.11
  1171.0 3.7 bitcast_add_fusion.11
  1183.5 3.7 bitcast_add_fusion.11
  1195.9 3.7 bitcast_add_fusion.11
  1208.4 3.7 bitcast_add_fusion.11
  1220.8 3.7 bitcast_add_fusion.11
  1233.2 3.7 bitcast_add_fusion.11
  1245.7 3.7 bitcast_add_fusion.11
  1258.1 3.7 bitcast_add_fusion.11
  1270.6 3.7 bitcast_add_fusion.11
  1283.0 3.7 bitcast_add_fusion.11
  1295.5 3.7 bitcast_add_fusion.11
  1305.4 5.9 add_bitcast_fusion
  1314.1 11.7 reduce-scatter.2.cloned.1.call-done
  (596 shorter events, 717.3 us)
Async XLA Ops:
  7.2 269.0 %all-gather.5.cloned.1.call-start = ((), (), s32[]{:S(2)}) async-start(), calls=%async_computation.2 | async-start | bytes 1310720 | tf_op jit(solution)/shard_map/all_gather | solution.py:103
  7.2 53.6 %collective-permute-start = (bf16[1,56,128,128]{3,2,1,0:T(8,128)(2,1)}, bf16[1,56,128,128]{3,2,1,0:T(8,128)(2,1)S(1)}, u32[]{:S(2)}, u32[]{:S(2)}) collective-permute-start(bf16[1,56,128,128]{3,2,1,0:T(8,128)(2,1)} %param.31), channel_id=1, source_target_pairs={{0,4},{4,8},{8,12},{12,16},{16,20},{20,24},{24,28},{28,0},{1,5},{5... | collective-permute-start | bytes 5505032 | tf_op jit(solution)/shard_map/ppermute | solution.py:21
  12.0 608.6 %all-gather.3.cloned.1.call-start = ((), (), s32[]{:S(2)}) async-start(), calls=%async_computation.1 | async-start | bytes 16515072 | tf_op jit(solution)/shard_map/all_gather | solution.py:108
  12.8 1313.0 %reduce-scatter.2.cloned.1.call-start = ((), (), s32[]{:S(2)}) async-start(), calls=%async_computation.3 | async-start | bytes 1310720 | tf_op jit(solution)/shard_map/reduce_scatter | solution.py:140
  60.8 87.2 %collective-permute-start.1 = (bf16[1,56,128,128]{3,2,1,0:T(8,128)(2,1)S(1)}, bf16[1,56,128,128]{3,2,1,0:T(8,128)(2,1)S(1)}, u32[]{:S(2)}, u32[]{:S(2)}) collective-permute-start(bf16[1,56,128,128]{3,2,1,0:T(8,128)(2,1)S(1)} %collective-permute-done), channel_id=1, source_target_pairs={{0,4},{4,8},{8,12},{12,16},{16,20},{20,24},{24,28},{28,0},{1,5},{5... | collective-permute-start | bytes 5505032 | tf_op jit(solution)/shard_map/ppermute | solution.py:21
  61.5 90.4 %collective-permute-start.4 = (bf16[1,56,128,128]{3,2,1,0:T(8,128)(2,1)}, bf16[1,56,128,128]{3,2,1,0:T(8,128)(2,1)}, u32[]{:S(2)}, u32[]{:S(2)}) collective-permute-start(bf16[1,56,128,128]{3,2,1,0:T(8,128)(2,1)} %param.31), channel_id=1, source_target_pairs={{4,0},{8,4},{12,8},{16,12},{20,16},{24,20},{28,24},{0,28},{5,1},{9... | collective-permute-start | bytes 5505032 | tf_op jit(solution)/shard_map/ppermute | solution.py:23
  148.0 1.2 copy-start.11
  149.2 119.7 %collective-permute-start.2 = (bf16[1,56,128,128]{3,2,1,0:T(8,128)(2,1)S(1)}, bf16[1,56,128,128]{3,2,1,0:T(8,128)(2,1)}, u32[]{:S(2)}, u32[]{:S(2)}) collective-permute-start(bf16[1,56,128,128]{3,2,1,0:T(8,128)(2,1)S(1)} %collective-permute-done.1), channel_id=1, source_target_pairs={{0,4},{4,8},{8,12},{12,16},{16,20},{20,24},{24,28},{28,0},{1,5},{5... | collective-permute-start | bytes 5505032 | tf_op jit(solution)/shard_map/ppermute | solution.py:21
  151.9 127.2 %collective-permute-start.5 = (bf16[1,56,128,128]{3,2,1,0:T(8,128)(2,1)}, bf16[1,56,128,128]{3,2,1,0:T(8,128)(2,1)}, u32[]{:S(2)}, u32[]{:S(2)}) collective-permute-start(bf16[1,56,128,128]{3,2,1,0:T(8,128)(2,1)} %collective-permute-done.4), channel_id=1, source_target_pairs={{4,0},{8,4},{12,8},{16,12},{20,16},{24,20},{28,24},{0,28},{5,1},{9... | collective-permute-start | bytes 5505032 | tf_op jit(solution)/shard_map/ppermute | solution.py:23
  269.0 119.4 %collective-permute-start.3 = (bf16[1,56,128,128]{3,2,1,0:T(8,128)(2,1)}, bf16[1,56,128,128]{3,2,1,0:T(8,128)(2,1)}, u32[]{:S(2)}, u32[]{:S(2)}) collective-permute-start(bf16[1,56,128,128]{3,2,1,0:T(8,128)(2,1)} %collective-permute-done.2), channel_id=1, source_target_pairs={{0,4},{4,8},{8,12},{12,16},{16,20},{20,24},{24,28},{28,0},{1,5},{5... | collective-permute-start | bytes 5505032 | tf_op jit(solution)/shard_map/ppermute | solution.py:21
  278.5 113.5 %copy-start.12 = (bf16[1,56,128,128]{3,2,1,0:T(8,128)(2,1)S(1)}, bf16[1,56,128,128]{3,2,1,0:T(8,128)(2,1)}, u32[]{:S(2)}) copy-start(bf16[1,56,128,128]{3,2,1,0:T(8,128)(2,1)} %copy-done.11) | copy-start | bytes 5505028
  278.5 548.6 %collective-permute-start.7 = (bf16[128,32,128]{2,0,1:T(8,128)(2,1)}, bf16[128,32,128]{2,0,1:T(8,128)(2,1)}, u32[]{:S(2)}, u32[]{:S(2)}) collective-permute-start(bf16[128,32,128]{2,0,1:T(8,128)(2,1)} %copy.98), channel_id=1, source_target_pairs={{0,4},{4,0},{8,12},{12,8},{16,20},{20,16},{24,28},{28,24},{1,5},{5... | collective-permute-start | bytes 3145736 | tf_op jit(solution)/shard_map/ppermute | solution.py:33
  279.1 132.9 %collective-permute-start.6 = (bf16[1,56,128,128]{3,2,1,0:T(8,128)(2,1)}, bf16[1,56,128,128]{3,2,1,0:T(8,128)(2,1)S(1)}, u32[]{:S(2)}, u32[]{:S(2)}) collective-permute-start(bf16[1,56,128,128]{3,2,1,0:T(8,128)(2,1)} %collective-permute-done.5), channel_id=1, source_target_pairs={{4,0},{8,4},{12,8},{16,12},{20,16},{24,20},{28,24},{0,28},{5,1},{9... | collective-permute-start | bytes 5505032 | tf_op jit(solution)/shard_map/ppermute | solution.py:23
  392.0 1.6 copy-start.10
  412.3 5.2 copy-start.8
  417.5 12.9 copy-start.2
  417.5 12.9 copy-start.3
  430.5 190.1 %copy-start = (s32[1,448]{1,0:T(1,128)S(1)}, s32[1,448]{1,0:T(1,128)}, u32[]{:S(2)}) copy-start(s32[1,448]{1,0:T(1,128)} %param.33) | copy-start | bytes 5380
  430.5 190.1 %copy-start.1 = (s32[1,448]{1,0:T(1,128)S(1)}, s32[1,448]{1,0:T(1,128)}, u32[]{:S(2)}) copy-start(s32[1,448]{1,0:T(1,128)} %param.32) | copy-start | bytes 5380
  817.1 41.7 %copy-start.4 = (bf16[128,28,128]{2,0,1:T(8,128)(2,1)}, bf16[128,28,128]{2,0,1:T(8,128)(2,1)S(1)}, u32[]{:S(2)}) copy-start(bf16[128,28,128]{2,0,1:T(8,128)(2,1)S(1)} %get-tuple-element.1286) | copy-start | bytes 2752516
  817.1 30.4 %collective-permute-start.8 = (bf16[128,28,128]{2,0,1:T(8,128)(2,1)}, bf16[128,28,128]{2,0,1:T(8,128)(2,1)}, u32[]{:S(2)}, u32[]{:S(2)}) collective-permute-start(bf16[128,28,128]{2,0,1:T(8,128)(2,1)} %get-tuple-element.1253), channel_id=1, source_target_pairs={{0,4},{4,0},{8,12},{12,8},{16,20},{20,16},{24,28},{28,24},{1,5},{5... | collective-permute-start | bytes 2752520 | tf_op jit(solution)/shard_map/ppermute | solution.py:33
  825.0 33.8 %collective-permute-start.9 = (bf16[128,28,128]{2,0,1:T(8,128)(2,1)S(1)}, bf16[128,28,128]{2,0,1:T(8,128)(2,1)}, u32[]{:S(2)}, u32[]{:S(2)}) collective-permute-start(bf16[128,28,128]{2,0,1:T(8,128)(2,1)S(1)} %get-tuple-element.1286), channel_id=1, source_target_pairs={{0,4},{4,0},{8,12},{12,8},{16,20},{20,16},{24,28},{28,24},{1,5},{5... | collective-permute-start | bytes 2752520 | tf_op jit(solution)/shard_map/ppermute | solution.py:33
  916.1 189.2 %collective-permute-start.10 = (bf16[2,56,2,128,128]{4,3,1,2,0:T(8,128)(2,1)}, bf16[2,56,2,128,128]{4,3,1,2,0:T(8,128)(2,1)}, u32[]{:S(2)}, u32[]{:S(2)}) collective-permute-start(bf16[2,56,2,128,128]{4,3,1,2,0:T(8,128)(2,1)} %fusion.115), channel_id=1, source_target_pairs={{0,8},{4,12},{8,0},{12,4},{16,24},{20,28},{24,16},{28,20},{1,9},{5... | collective-permute-start | bytes 22020104 | tf_op jit(solution)/shard_map/ppermute | solution.py:33
  1113.9 5.2 copy-start.7
  1119.1 6.5 copy-start.5
  1121.8 183.6 %collective-permute-start.11 = (bf16[1,56,2,128,128]{4,3,1,2,0:T(8,128)(2,1)}, bf16[1,56,2,128,128]{4,3,1,2,0:T(8,128)(2,1)}, u32[]{:S(2)}, u32[]{:S(2)}) collective-permute-start(bf16[1,56,2,128,128]{4,3,1,2,0:T(8,128)(2,1)} %dynamic-slice_convert_fusion), channel_id=1, source_target_pairs={{0,16},{4,20},{8,24},{12,28},{16,0},{20,4},{24,8},{28,12},{1,17},{... | collective-permute-start | bytes 11010056 | tf_op jit(solution)/shard_map/ppermute | solution.py:33
  1134.3 3.1 copy-start.6
  1146.1 3.7 copy-start.6
  1158.6 3.7 copy-start.6
  1171.0 3.7 copy-start.6
  1183.5 3.7 copy-start.6
  1195.9 3.7 copy-start.6
  1208.3 3.7 copy-start.6
  1220.8 3.7 copy-start.6
  1233.2 3.7 copy-start.6
  1245.7 3.7 copy-start.6
  1258.1 3.7 copy-start.6
  1270.6 3.7 copy-start.6
  1283.0 3.7 copy-start.6
  1295.5 3.7 copy-start.6
  1299.2 4.3 copy-start.9
Sparse Core Ops, SparseCore 0:
  12.2 17.3 all-gather.4
  31.8 401.0 all-gather.2
  1303.6 22.1 reduce-scatter.1
